TPU v7x, 32 devices: a whole 2x2x4 slice. The times are simulated.
32 devices in a mesh: member: 4 (over x, core), space: 8 (over z, y).
Axes of the slice: x: 2, y: 2, z: 4, core: 2. Of those that a mesh axis runs over, the one named last changes fastest.
Arguments:
- features: bfloat16 [4, 641, 192, 128], P('member', None, 'space'), may hold values from -6 to 6
- depth_kernel: float32 [641, 5, 5], replicated, may hold values from -1.25 to 1.25
- in_weight: bfloat16 [641, 1282], replicated, may hold values from -0.25 to 0.25
- out_weight: bfloat16 [1282, 641], replicated, may hold values from -0.15625 to 0.15625
- decoder_weight: bfloat16 [641, 72], replicated, may hold values from -0.25 to 0.25
- observed: float32 [72, 192, 128], P(None, 'space'), may hold values from -6 to 6
- land_mask: int32 [192, 128], P('space'), may hold values 0 or 1
Outputs:
- grad_features: bfloat16 [4, 641, 192, 128], P('member', None, 'space')
- decoder_grad: float32 [641, 72], replicated
All inputs are finite; a program needn't handle non-finite values. No bound on the sum of `land_mask` on one device may be relied on, other than what follows from the above.
Results may differ from a plain program's by a relative error of at most 0.0054.
Values may be sent and summed in bfloat16 or wider, within the bound.
A program may use at most 128 MiB of HBM per device.

v0:
```python
import math
import jax
import jax.numpy as jnp
from jax import lax
from jax.sharding import PartitionSpec as P

norm_eps = 1e-05


def padded_2(cells, sides, width):
    for axis, dim in sides:
        count = lax.axis_size(axis)
        head = lax.slice_in_dim(cells, 0, width, axis=dim)
        tail = lax.slice_in_dim(cells, cells.shape[dim] - width, cells.shape[dim], axis=dim)
        cells = jnp.concatenate(
            [
                lax.ppermute(tail, axis, [(i, (i + 1) % count) for i in range(count)]),
                cells,
                lax.ppermute(head, axis, [((i + 1) % count, i) for i in range(count)]),
            ],
            axis=dim,
        )
    return cells


def per_device(features, depth_kernel, in_weight, out_weight, decoder_weight, observed, land_mask):
    channels = features.shape[1]
    lon_len = features.shape[2]
    lat_len = features.shape[3]
    points = lon_len * lat_len
    padded = padded_2(features, (("space", 2),), 2)
    widened = jnp.pad(padded.astype(jnp.float32), ((0, 0), (0, 0), (0, 0), (2, 2)))
    convolved = jnp.zeros(features.shape, jnp.float32)
    for row_off in range(5):
        for col_off in range(5):
            convolved = (
                convolved
                + depth_kernel[:, row_off, col_off][None, :, None, None]
                * widened[:, :, row_off : row_off + lon_len, col_off : col_off + lat_len]
            )
    center = jnp.mean(convolved, axis=1, keepdims=True)
    shifted = convolved - center
    normed = (
        shifted * lax.rsqrt(jnp.mean(shifted * shifted, axis=1, keepdims=True) + norm_eps)
    ).astype(jnp.bfloat16)
    flat = normed.reshape(channels, points)
    hidden = jax.nn.gelu(
        jnp.einsum("ch,cp->hp", in_weight, flat, preferred_element_type=jnp.float32),
        approximate=False,
    ).astype(jnp.bfloat16)
    mlp_out = jnp.einsum("hc,hp->cp", out_weight, hidden, preferred_element_type=jnp.float32)
    block_out = (features.reshape(channels, points).astype(jnp.float32) + mlp_out).astype(
        jnp.bfloat16
    )
    decoded_flat = jnp.einsum(
        "co,cp->op", decoder_weight, block_out, preferred_element_type=jnp.float32
    ).astype(jnp.bfloat16)
    outputs = decoded_flat.shape[0]
    decoded = decoded_flat.reshape(1, outputs, lon_len, lat_len)
    groups = lax.axis_size("member")
    members = features.shape[0] * groups
    point_weight = 4.0 + 8.0 * land_mask.astype(jnp.float32)
    own_f = decoded.astype(jnp.float32)
    apart = own_f - lax.all_gather(decoded, "member", axis=0, tiled=True).astype(jnp.float32)
    apart_norm = jnp.sqrt(jnp.sum(apart * apart, axis=1, keepdims=True) + 1.0)
    pair_sum = jnp.sum(apart / apart_norm, axis=0, keepdims=True)
    misfit = own_f - observed[None]
    misfit_norm = jnp.sqrt(jnp.sum(misfit * misfit, axis=1, keepdims=True) + 1.0)
    score_grad = (point_weight[None, None] * (misfit / misfit_norm - pair_sum / members)).astype(
        jnp.bfloat16
    )
    grad_flat = score_grad.reshape(outputs, points)
    grad_features = jnp.einsum(
        "co,op->cp", decoder_weight, grad_flat, preferred_element_type=jnp.float32
    ).astype(jnp.bfloat16)
    total_points = lon_len * lax.axis_size("space") * lat_len
    term = jnp.einsum(
        "cp,op->co", block_out, grad_flat, preferred_element_type=jnp.float32
    ) / math.sqrt(members * total_points)
    decoder_grad = lax.psum(term, ("member", "space"))
    return (grad_features.reshape(features.shape), decoder_grad)


def solution(mesh):
    placed = (
        P("member", None, "space", None),
        P(),
        P(),
        P(),
        P(),
        P(None, "space", None),
        P("space", None),
    )
    return jax.shard_map(
        per_device,
        mesh=mesh,
        in_specs=placed,
        out_specs=(P("member", None, "space", None), P()),
        check_vma=False,
    )
```

profile of v0, /device:TPU:8, one launch (start us, length us, event | category | flops | bytes accessed | tf_op | source)
XLA Modules:
  0.0 393.1 jit_solution(12034791294327075821)
XLA Ops:
  7.2 2.3 fusion.106
  9.6 1.6 collective-permute-start
  11.3 1.5 collective-permute-start.1
  12.7 2.6 convert_bitcast_fusion
  15.3 0.5 pad.8
  15.9 5.0 %copy.15 = f32[81,8,24,128]{3,1,2,0:T(8,128)} copy(f32[81,8,24,128]{3,2,1,0:T(8,128)S(1)} %bitcast.131) | data formatting | bytes 15925248
  21.1 4.2 %collective-permute-done = bf16[1,641,2,128]{3,1,2,0:T(8,128)(2,1)S(1)} collective-permute-done((bf16[1,641,2,128]{3,1,2,0:T(8,128)(2,1)S(1)}, bf16[1,641,2,128]{3,1,2,0:T(8,128)(2,1)S(1)}, u32[]{:S(2)}, u32[]{:S(2)}) %collective-permute-start) | collective-permute-done | bytes 328224 | tf_op jit(solution)/shard_map/ppermute | solution.py:17
  25.4 0.3 copy.11
  25.6 1.6 collective-permute-done.1
  27.2 0.3 copy.12
  27.5 6.9 %maximum_convert_fusion = f32[1,641,28,128]{3,2,1,0:T(8,128)} fusion(bf16[1,641,2,128]{3,2,1,0:T(2,128)(2,1)S(1)} %copy.12, bf16[1,641,24,128]{3,2,1,0:T(8,128)(2,1)S(1)} %copy-done.5, bf16[1,641,2,128]{3,2,1,0:T(2,128)(2,1)S(1)} %copy.11), kind=kLoop, calls=%fused_computation.100 | loop fusion | flops 13784064 | bytes 13784064 | tf_op jit(solution)/shard_map/convert_element_type | solution.py:32
  34.4 130.6 %fusion.104 = (f32[24,128]{1,0:T(8,128)S(1)}, f32[1,641,24,128]{3,2,1,0:T(8,128)}) fusion(f32[641]{0:T(1024)S(1)} %get-tuple-element.25, f32[641]{0:T(1024)S(1)} %get-tuple-element.26, f32[1,641,28,128]{3,2,1,0:T(8,128)} %maximum_convert_fusion, f32[641]{0:T(1024)S(1)} %get-tuple-element.3, f32[641]{0:T(1024)S(1)} %get-tuple-element.4, ...), kind=kLoop, calls=%fused_computation.177 | loop fusion | flops 98454528 | bytes 57838180 | tf_op jit(solution)/shard_map/reduce_sum | solution.py:41
  165.0 4.3 %multiply_reduce_fusion = f32[24,128]{1,0:T(8,128)S(1)} fusion(f32[1,641,24,128]{3,2,1,0:T(8,128)} %get-tuple-element.28, f32[24,128]{1,0:T(8,128)S(1)} %broadcast_multiply_fusion), kind=kLoop, calls=%fused_computation.99 | loop fusion | flops 5904384 | bytes 7901184 | tf_op jit(solution)/shard_map/reduce_sum | solution.py:44
  169.3 1.1 copy-done.2
  170.4 0.9 fusion.69
  171.3 0.7 pad.9
  172.0 1.1 copy.16
  173.2 42.9 %fusion.123 = bf16[1282,3072]{1,0:T(8,128)(2,1)S(1)} fusion(bf16[641,3072]{1,0:T(8,128)(2,1)S(1)} %bitcast.142, bf16[641,1282]{1,0:T(8,128)(2,1)S(1)} %copy-done), kind=kOutput, calls=%fused_computation.23.clone.clone.clone.clone.1 | convolution fusion | flops 5304895488 | bytes 13458436 | tf_op jit(solution)/shard_map/ch,cp->hp/dot_general | solution.py:48
  216.2 7.2 %fusion.18 = bf16[641,3072]{1,0:T(8,128)(2,1)S(1)} fusion(f32[641,3072]{1,0:T(8,128)S(1)} %bitcast.138, bf16[1282,641]{0,1:T(8,128)(2,1)S(1)} %copy-done.10, bf16[1282,3072]{1,0:T(8,128)(2,1)S(1)} %fusion.123), kind=kOutput, calls=%fused_computation.45 | convolution fusion | flops 5052844032 | bytes 21335044 | tf_op jit(solution)/shard_map/hc,hp->cp/dot_general | solution.py:51
  223.4 1.9 copy-done.3
  225.3 0.8 convolution_convert_fusion.1
  226.1 0.8 copy.18
  227.4 20.9 %all-gather.2.cloned.1.call-done = bf16[4,72,24,128]{3,2,1,0:T(8,128)(2,1)} async-done(((bf16[1,72,24,128]{3,2,1,0:T(8,128)(2,1)}), bf16[4,72,24,128]{3,2,1,0:T(8,128)(2,1)}) %all-gather.2.cloned.1.call-update) | async-done | bytes 1769488 | tf_op jit(solution)/shard_map/all_gather | solution.py:64
  248.4 2.1 multiply_reduce_fusion.1
  250.5 2.0 divide_reduce_fusion
  252.5 0.2 multiply_convert_fusion.1
  252.7 2.0 convolution_multiply_fusion
  254.7 3.1 convolution_convert_fusion
  257.9 3.4 copy.20
  261.3 2.6 slice_bitcast_fusion
  263.9 120.7 %all-reduce.3.cloned.1.call-done = f32[641,72]{0,1:T(8,128)} async-done(((f32[641,72]{0,1:T(8,128)}), f32[641,72]{0,1:T(8,128)}) %all-reduce.3.cloned.1.call-update) | async-done | bytes 184624 | tf_op jit(solution)/shard_map/psum | solution.py:80
  384.6 1.6 copy.30
  (40 shorter events, 0.9 us)
Async XLA Ops:
  7.2 166.0 %copy-start = (bf16[641,1282]{1,0:T(8,128)(2,1)S(1)}, bf16[641,1282]{1,0:T(8,128)(2,1)}, u32[]{:S(2)}) copy-start(bf16[641,1282]{1,0:T(8,128)(2,1)} %param.9) | copy-start | bytes 4930576
  7.2 241.2 %all-gather.2.cloned.1.call-start = ((), (), s32[]{:S(2)}) async-start(), calls=%async_computation | async-start | bytes 2211840 | tf_op jit(solution)/shard_map/all_gather | solution.py:64
  9.6 15.7 %collective-permute-start = (bf16[1,641,2,128]{3,1,2,0:T(8,128)(2,1)S(1)}, bf16[1,641,2,128]{3,1,2,0:T(8,128)(2,1)S(1)}, u32[]{:S(2)}, u32[]{:S(2)}) collective-permute-start(bf16[1,641,2,128]{3,1,2,0:T(8,128)(2,1)S(1)} %copy.13), channel_id=1, source_target_pairs={{0,1},{1,2},{2,3},{3,4},{4,5},{5,6},{6,7},{7,0},{8,9},{9,10},{10,1... | collective-permute-start | bytes 984584 | tf_op jit(solution)/shard_map/ppermute | solution.py:17
  11.3 16.0 %collective-permute-start.1 = (bf16[1,641,2,128]{3,1,2,0:T(8,128)(2,1)S(1)}, bf16[1,641,2,128]{3,1,2,0:T(8,128)(2,1)S(1)}, u32[]{:S(2)}, u32[]{:S(2)}) collective-permute-start(bf16[1,641,2,128]{3,1,2,0:T(8,128)(2,1)S(1)} %copy.14), channel_id=1, source_target_pairs={{1,0},{2,1},{3,2},{4,3},{5,4},{6,5},{7,6},{0,7},{9,8},{10,9},{11,1... | collective-permute-start | bytes 984584 | tf_op jit(solution)/shard_map/ppermute | solution.py:19
  15.9 5.0 %copy-start.8 = (f32[641,5,5]{0,2,1:T(8,128)S(1)}, f32[641,5,5]{0,2,1:T(8,128)}, u32[]{:S(2)}) copy-start(f32[641,5,5]{0,2,1:T(8,128)} %param.8) | copy-start | bytes 192304
  15.9 11.6 %copy-start.5 = (bf16[1,641,24,128]{3,2,1,0:T(8,128)(2,1)S(1)}, bf16[1,641,24,128]{3,2,1,0:T(8,128)(2,1)}, u32[]{:S(2)}) copy-start(bf16[1,641,24,128]{3,2,1,0:T(8,128)(2,1)} %param.7) | copy-start | bytes 11814916
  164.9 5.5 %copy-start.2 = (f32[1,641,24,128]{3,2,1,0:T(8,128)S(1)}, f32[1,641,24,128]{3,2,1,0:T(8,128)}, u32[]{:S(2)}) copy-start(f32[1,641,24,128]{3,2,1,0:T(8,128)} %get-tuple-element.28) | copy-start | bytes 23629828
  172.0 44.1 %slice-start = ((s8[7962624]{0:T(1024)(128)(4,1)}), s8[4194304]{0:T(1024)(128)(4,1)S(1)}, s32[]{:S(2)}) async-start(s8[7962624]{0:T(1024)(128)(4,1)} %bitcast.136), calls=%async_computation.2 | async-start | bytes 8388608
  173.1 43.0 %slice-start.1 = ((s8[7962624]{0:T(1024)(128)(4,1)}), s8[3768320]{0:T(1024)(128)(4,1)S(1)}, s32[]{:S(2)}) async-start(s8[7962624]{0:T(1024)(128)(4,1)} %bitcast.136), calls=%async_computation.3 | async-start | bytes 7536640
  173.2 43.0 %copy-start.10 = (bf16[1282,641]{0,1:T(8,128)(2,1)S(1)}, bf16[1282,641]{0,1:T(8,128)(2,1)}, u32[]{:S(2)}) copy-start(bf16[1282,641]{0,1:T(8,128)(2,1)} %param.10) | copy-start | bytes 4930576
  216.1 9.1 %copy-start.7 = (bf16[641,72]{0,1:T(8,128)(2,1)S(1)}, bf16[641,72]{0,1:T(8,128)(2,1)}, u32[]{:S(2)}) copy-start(bf16[641,72]{0,1:T(8,128)(2,1)} %param.11) | copy-start | bytes 276916
  223.4 1.9 copy-start.3
  225.3 1.9 copy-start.6
  225.3 2.1 copy-start.9
  226.9 157.7 %all-reduce.3.cloned.1.call-start = ((), (), s32[]{:S(2)}) async-start(), calls=%async_computation.1 | async-start | bytes 442368 | tf_op jit(solution)/shard_map/psum | solution.py:80
  248.3 4.4 %copy-start.4 = (bf16[641,3072]{1,0:T(8,128)(2,1)S(1)}, bf16[641,3072]{1,0:T(8,128)(2,1)}, u32[]{:S(2)}) copy-start(bf16[641,3072]{1,0:T(8,128)(2,1)} %copy-done.3) | copy-start | bytes 11814916
  257.9 128.3 %copy-start.1 = (bf16[641,1282]{1,0:T(8,128)(2,1)S(1)}, bf16[641,1282]{1,0:T(8,128)(2,1)}, u32[]{:S(2)}) copy-start(bf16[641,1282]{1,0:T(8,128)(2,1)} %param.9) | copy-start | bytes 4930576
Sparse Core Ops, SparseCore 0:
  227.0 21.2 all-gather.1
  258.0 126.5 all-reduce.2
where the time goes:
time: 393 us
  other arithmetic  150 us (38%)
  waiting for transfers between devices  148 us (38%)
  matrix products  56.1 us (14%)
  local copies, waits for them, and re-layouts  22.2 us (6%)
  between operations  14.3 us (4%)
    reduce_sum x1, other arithmetic, per_device(): center = jnp.mean(convolved, axis=1, keepdims=True)  131 us
    psum x1, waiting for transfers between devices, per_device(): decoder_grad = lax.psum(term, ('member', 'space'))  121 us
    dot_general x1, matrix products, per_device(): jnp.einsum('ch,cp->hp', in_weight, flat, preferred_element_type=jnp.float32)  42.9 us
    all_gather x1, waiting for transfers between devices, per_device(): lax.all_gather(decoded, 'member', axis=0, tiled=True).astype(jnp.float32)  20.9 us
    unnamed x36, local copies, waits for them, and re-layouts  16.6 us
  transfers between devices with their start and end apart: 4, of which 4 were waited for; matrix products, arithmetic and copies ran while one was open for 4% of the time, Pallas kernels for 0%

commit v1 on v0

--- a/solution.py
+++ b/solution.py
@@ -77,7 +77,7 @@
     term = jnp.einsum(
         "cp,op->co", block_out, grad_flat, preferred_element_type=jnp.float32
     ) / math.sqrt(members * total_points)
-    decoder_grad = lax.psum(term, ("member", "space"))
+    decoder_grad = jnp.sum(lax.all_gather(term, ("member", "space")), axis=0)
     return (grad_features.reshape(features.shape), decoder_grad)
 
 

time: 393 us -> 340 us (0.87)
  waiting for transfers between devices: 148 us -> 94 us
  other arithmetic: 150 us -> 154 us
    psum x1 -> x0, waiting for transfers between devices: 121 us -> none  [per_device(): decoder_grad = lax.psum(term, ('member', 'space'))]
    all_gather x0 -> x1, waiting for transfers between devices: none -> 67.1 us  [per_device(): decoder_grad = jnp.sum(lax.all_gather(term, ('member', 'space')), axis=0)]
    reduce_sum x0 -> x1, other arithmetic: none -> 4.07 us  [per_device(): decoder_grad = jnp.sum(lax.all_gather(term, ('member', 'space')), axis=0)]
    unnamed x36 -> x35, local copies, waits for them, and re-layouts: 16.6 us -> 12.7 us
where the time goes in v1:
time: 340 us; the launch traced here: 338 us
  other arithmetic  154 us (45%)
  waiting for transfers between devices  94 us (28%)
  matrix products  54.2 us (16%)
  local copies, waits for them, and re-layouts  18.3 us (5%)
  between operations  14.3 us (4%)
    reduce_sum x1, other arithmetic, per_device(): center = jnp.mean(convolved, axis=1, keepdims=True)  131 us
    all_gather x1, waiting for transfers between devices, per_device(): decoder_grad = jnp.sum(lax.all_gather(term, ('member', 'space')), axis=0)  67.1 us
    dot_general x1, matrix products, per_device(): jnp.einsum('ch,cp->hp', in_weight, flat, preferred_element_type=jnp.float32)  42.9 us
    all_gather x1, waiting for transfers between devices, per_device(): lax.all_gather(decoded, 'member', axis=0, tiled=True).astype(jnp.float32)  20.9 us
    unnamed x35, local copies, waits for them, and re-layouts  12.7 us
    dot_general x1, matrix products, per_device(): jnp.einsum('hc,hp->cp', out_weight, hidden, preferred_element_type=jnp.fl...  7.22 us
    convert_element_type x1, other arithmetic, per_device(): padded.astype(jnp.float32)  6.88 us
  transfers between devices with their start and end apart: 4, of which 4 were waited for; matrix products, arithmetic and copies ran while one was open for 4% of the time, Pallas kernels for 0%

profile of v1, /device:TPU:8, one launch (start us, length us, event | category | flops | bytes accessed | tf_op | source)
XLA Modules:
  0.0 337.8 jit_solution(8393234483265893448)
XLA Ops:
  7.2 2.3 fusion.107
  9.6 1.6 collective-permute-start
  11.3 1.5 collective-permute-start.1
  12.7 2.6 convert_bitcast_fusion
  15.3 0.5 pad.8
  15.9 5.0 %copy.15 = f32[81,8,24,128]{3,1,2,0:T(8,128)} copy(f32[81,8,24,128]{3,2,1,0:T(8,128)S(1)} %bitcast.133) | data formatting | bytes 15925248
  21.1 4.2 %collective-permute-done = bf16[1,641,2,128]{3,1,2,0:T(8,128)(2,1)S(1)} collective-permute-done((bf16[1,641,2,128]{3,1,2,0:T(8,128)(2,1)S(1)}, bf16[1,641,2,128]{3,1,2,0:T(8,128)(2,1)S(1)}, u32[]{:S(2)}, u32[]{:S(2)}) %collective-permute-start) | collective-permute-done | bytes 328224 | tf_op jit(solution)/shard_map/ppermute | solution.py:17
  25.4 0.3 copy.11
  25.6 1.6 collective-permute-done.1
  27.2 0.3 copy.12
  27.5 6.9 %maximum_convert_fusion = f32[1,641,28,128]{3,2,1,0:T(8,128)} fusion(bf16[1,641,2,128]{3,2,1,0:T(2,128)(2,1)S(1)} %copy.12, bf16[1,641,24,128]{3,2,1,0:T(8,128)(2,1)S(1)} %copy-done.5, bf16[1,641,2,128]{3,2,1,0:T(2,128)(2,1)S(1)} %copy.11), kind=kLoop, calls=%fused_computation.100 | loop fusion | flops 13784064 | bytes 13784064 | tf_op jit(solution)/shard_map/convert_element_type | solution.py:32
  34.4 130.5 %fusion.105 = (f32[24,128]{1,0:T(8,128)S(1)}, f32[1,641,24,128]{3,2,1,0:T(8,128)}) fusion(f32[641]{0:T(1024)S(1)} %get-tuple-element.25, f32[641]{0:T(1024)S(1)} %get-tuple-element.26, f32[1,641,28,128]{3,2,1,0:T(8,128)} %maximum_convert_fusion, f32[641]{0:T(1024)S(1)} %get-tuple-element.3, f32[641]{0:T(1024)S(1)} %get-tuple-element.4, ...), kind=kLoop, calls=%fused_computation.178 | loop fusion | flops 98454528 | bytes 57838180 | tf_op jit(solution)/shard_map/reduce_sum | solution.py:41
  164.9 4.3 %multiply_reduce_fusion = f32[24,128]{1,0:T(8,128)S(1)} fusion(f32[1,641,24,128]{3,2,1,0:T(8,128)} %get-tuple-element.28, f32[24,128]{1,0:T(8,128)S(1)} %broadcast_multiply_fusion), kind=kLoop, calls=%fused_computation.99 | loop fusion | flops 5904384 | bytes 7901184 | tf_op jit(solution)/shard_map/reduce_sum | solution.py:44
  169.2 1.1 copy-done.2
  170.4 0.9 fusion.69
  171.2 0.7 pad.9
  171.9 1.2 copy.16
  173.1 42.9 %fusion.124 = bf16[1282,3072]{1,0:T(8,128)(2,1)S(1)} fusion(bf16[641,3072]{1,0:T(8,128)(2,1)S(1)} %bitcast.144, bf16[641,1282]{1,0:T(8,128)(2,1)S(1)} %copy-done), kind=kOutput, calls=%fused_computation.23.clone.clone.clone.clone.1 | convolution fusion | flops 5304895488 | bytes 13458436 | tf_op jit(solution)/shard_map/ch,cp->hp/dot_general | solution.py:48
  216.1 7.2 %fusion.18 = bf16[641,3072]{1,0:T(8,128)(2,1)S(1)} fusion(f32[641,3072]{1,0:T(8,128)S(1)} %bitcast.140, bf16[1282,641]{0,1:T(8,128)(2,1)S(1)} %copy-done.10, bf16[1282,3072]{1,0:T(8,128)(2,1)S(1)} %fusion.124), kind=kOutput, calls=%fused_computation.45 | convolution fusion | flops 5052844032 | bytes 21335044 | tf_op jit(solution)/shard_map/hc,hp->cp/dot_general | solution.py:51
  223.4 1.9 copy-done.3
  225.2 0.8 convolution_convert_fusion.1
  226.0 0.8 copy.18
  227.4 20.9 %all-gather.5.cloned.1.call-done = bf16[4,72,24,128]{3,2,1,0:T(8,128)(2,1)} async-done(((bf16[1,72,24,128]{3,2,1,0:T(8,128)(2,1)}), bf16[4,72,24,128]{3,2,1,0:T(8,128)(2,1)}) %all-gather.5.cloned.1.call-update) | async-done | bytes 1769488 | tf_op jit(solution)/shard_map/all_gather | solution.py:64
  248.3 2.1 multiply_reduce_fusion.1
  250.4 2.0 divide_reduce_fusion
  252.5 0.2 multiply_convert_fusion.1
  252.7 2.0 fusion.70
  254.7 1.2 convolution_convert_fusion
  256.0 1.2 copy.20
  257.1 2.6 slice_bitcast_fusion
  259.8 67.1 %all-gather.7.cloned.1.call-done = f32[32,641,72]{1,2,0:T(8,128)} async-done(((f32[1,641,72]{1,2,0:T(8,128)}), f32[32,641,72]{1,2,0:T(8,128)}) %all-gather.7.cloned.1.call-update) | async-done | bytes 5907472 | tf_op jit(solution)/shard_map/all_gather | solution.py:80
  326.9 4.1 %reduce_sum.59 = f32[641,72]{0,1:T(8,128)} reduce(f32[32,641,72]{1,2,0:T(8,128)} %all-gather.7.cloned.1.call-done, f32[]{:T(128)} %constant.38.clone.1), dimensions={0}, to_apply=%region_5.6 | reduce | flops 1430712 | bytes 6092068 | tf_op jit(solution)/shard_map/reduce_sum | solution.py:80
  (40 shorter events, 0.9 us)
Async XLA Ops:
  7.2 165.9 %copy-start = (bf16[641,1282]{1,0:T(8,128)(2,1)S(1)}, bf16[641,1282]{1,0:T(8,128)(2,1)}, u32[]{:S(2)}) copy-start(bf16[641,1282]{1,0:T(8,128)(2,1)} %param.9) | copy-start | bytes 4930576
  7.2 241.1 %all-gather.5.cloned.1.call-start = ((), (), s32[]{:S(2)}) async-start(), calls=%async_computation | async-start | bytes 2211840 | tf_op jit(solution)/shard_map/all_gather | solution.py:64
  9.6 15.7 %collective-permute-start = (bf16[1,641,2,128]{3,1,2,0:T(8,128)(2,1)S(1)}, bf16[1,641,2,128]{3,1,2,0:T(8,128)(2,1)S(1)}, u32[]{:S(2)}, u32[]{:S(2)}) collective-permute-start(bf16[1,641,2,128]{3,1,2,0:T(8,128)(2,1)S(1)} %copy.13), channel_id=1, source_target_pairs={{0,1},{1,2},{2,3},{3,4},{4,5},{5,6},{6,7},{7,0},{8,9},{9,10},{10,1... | collective-permute-start | bytes 984584 | tf_op jit(solution)/shard_map/ppermute | solution.py:17
  11.3 16.0 %collective-permute-start.1 = (bf16[1,641,2,128]{3,1,2,0:T(8,128)(2,1)S(1)}, bf16[1,641,2,128]{3,1,2,0:T(8,128)(2,1)S(1)}, u32[]{:S(2)}, u32[]{:S(2)}) collective-permute-start(bf16[1,641,2,128]{3,1,2,0:T(8,128)(2,1)S(1)} %copy.14), channel_id=1, source_target_pairs={{1,0},{2,1},{3,2},{4,3},{5,4},{6,5},{7,6},{0,7},{9,8},{10,9},{11,1... | collective-permute-start | bytes 984584 | tf_op jit(solution)/shard_map/ppermute | solution.py:19
  15.9 5.0 %copy-start.8 = (f32[641,5,5]{0,2,1:T(8,128)S(1)}, f32[641,5,5]{0,2,1:T(8,128)}, u32[]{:S(2)}) copy-start(f32[641,5,5]{0,2,1:T(8,128)} %param.8) | copy-start | bytes 192304
  15.9 11.6 %copy-start.5 = (bf16[1,641,24,128]{3,2,1,0:T(8,128)(2,1)S(1)}, bf16[1,641,24,128]{3,2,1,0:T(8,128)(2,1)}, u32[]{:S(2)}) copy-start(bf16[1,641,24,128]{3,2,1,0:T(8,128)(2,1)} %param.7) | copy-start | bytes 11814916
  164.9 5.5 %copy-start.2 = (f32[1,641,24,128]{3,2,1,0:T(8,128)S(1)}, f32[1,641,24,128]{3,2,1,0:T(8,128)}, u32[]{:S(2)}) copy-start(f32[1,641,24,128]{3,2,1,0:T(8,128)} %get-tuple-element.28) | copy-start | bytes 23629828
  171.9 44.2 %slice-start = ((s8[7962624]{0:T(1024)(128)(4,1)}), s8[4194304]{0:T(1024)(128)(4,1)S(1)}, s32[]{:S(2)}) async-start(s8[7962624]{0:T(1024)(128)(4,1)} %bitcast.138), calls=%async_computation.2 | async-start | bytes 8388608
  173.1 43.0 %slice-start.1 = ((s8[7962624]{0:T(1024)(128)(4,1)}), s8[3768320]{0:T(1024)(128)(4,1)S(1)}, s32[]{:S(2)}) async-start(s8[7962624]{0:T(1024)(128)(4,1)} %bitcast.138), calls=%async_computation.3 | async-start | bytes 7536640
  173.1 43.0 %copy-start.10 = (bf16[1282,641]{0,1:T(8,128)(2,1)S(1)}, bf16[1282,641]{0,1:T(8,128)(2,1)}, u32[]{:S(2)}) copy-start(bf16[1282,641]{0,1:T(8,128)(2,1)} %param.10) | copy-start | bytes 4930576
  216.1 9.1 %copy-start.7 = (bf16[641,72]{0,1:T(8,128)(2,1)S(1)}, bf16[641,72]{0,1:T(8,128)(2,1)}, u32[]{:S(2)}) copy-start(bf16[641,72]{0,1:T(8,128)(2,1)} %param.11) | copy-start | bytes 276916
  223.4 1.9 copy-start.3
  225.2 1.9 copy-start.6
  225.2 2.1 copy-start.9
  226.9 100.0 %all-gather.7.cloned.1.call-start = ((), (), s32[]{:S(2)}) async-start(), calls=%async_computation.1 | async-start | bytes 7299072 | tf_op jit(solution)/shard_map/all_gather | solution.py:80
  248.3 4.4 %copy-start.4 = (bf16[641,3072]{1,0:T(8,128)(2,1)S(1)}, bf16[641,3072]{1,0:T(8,128)(2,1)}, u32[]{:S(2)}) copy-start(bf16[641,3072]{1,0:T(8,128)(2,1)} %copy-done.3) | copy-start | bytes 11814916
  256.0 75.0 %copy-start.1 = (bf16[641,1282]{1,0:T(8,128)(2,1)S(1)}, bf16[641,1282]{1,0:T(8,128)(2,1)}, u32[]{:S(2)}) copy-start(bf16[641,1282]{1,0:T(8,128)(2,1)} %param.9) | copy-start | bytes 4930576
Sparse Core Ops, SparseCore 0:
  227.0 21.2 all-gather.4
  254.9 71.9 all-gather.6
